TPU v7x, 256 devices: a whole 4x4x8 slice. The times are simulated.
256 devices in a mesh: dp: 32 (over x, y, core), ctx: 8 (over z).
Axes of the slice: x: 4, y: 4, z: 8, core: 2. Of those that a mesh axis runs over, the one named last changes fastest.
Arguments:
- cotangent: bfloat16 [32, 4096, 8192], P('dp', 'ctx'), may hold values from -6 to 6
- out_weight: bfloat16 [256, 8192], P(None, 'ctx'), may hold values from -0.0625 to 0.0625
- head_input: bfloat16 [32, 4096, 256], P('dp', 'ctx'), may hold values from -6 to 6
- injector: bfloat16 [32, 4096, 128], P('dp', 'ctx'), may hold values from -0.59765625 to 0.59765625
- readout: bfloat16 [32, 4096, 128], P('dp', 'ctx'), may hold values from -0.59765625 to 0.59765625
- decay_code: int32 [32, 4096, 2], P('dp', 'ctx'), may hold values from 1 to 40960
- decay_rate: float32 [2], replicated, may hold values from 4.8828125e-06 to 0.0061035156
- start_state: float32 [32, 8, 2, 128, 128], P('dp', 'ctx'), may hold values from -6 to 6
Outputs:
- gradient_input: bfloat16 [32, 4096, 256], P('dp', 'ctx')
- gradient_injector: float32 [32, 4096, 128], P('dp', 'ctx')
- gradient_readout: float32 [32, 4096, 128], P('dp', 'ctx')
- gradient_weight: float32 [256, 8192], P('ctx', 'dp')
- gradient_rate: float32 [2], replicated
All inputs are finite; a program needn't handle non-finite values.
Results may differ from a plain program's by a relative error of at most 0.0049.
Values may be sent and summed in bfloat16 or wider, within the bound.
No kernel may reach another device: no remote copies, remote signals or barrier semaphores. Data moves between devices by JAX's collectives and lax.ppermute only.
A program may use at most 128 MiB of HBM per device.

v0:
```python
import jax
import jax.numpy as jnp
from jax import lax
from jax.sharding import PartitionSpec as P

precise = lax.Precision.HIGHEST


def carried_in(value, axis, join, neutral):
    count, mine = (lax.axis_size(axis), lax.axis_index(axis))
    pieces = jax.tree.map(lambda part: lax.all_gather(part, axis), value)
    pieces = jax.tree.map(lambda part: part[::-1], pieces)
    mine = count - 1 - mine
    total = jax.tree.map(
        lambda part, zero: jnp.full_like(part, 0) + jnp.asarray(zero, part.dtype), value, neutral
    )

    def lap(position, total):
        longer = join(total, jax.tree.map(lambda part: part[position], pieces))
        return jax.tree.map(lambda new, old: jnp.where(position < mine, new, old), longer, total)

    return lax.fori_loop(0, count - 1, lap, total)


def decay_table(log_decay):
    cumulative = jnp.cumsum(log_decay, axis=0)
    length = log_decay.shape[0]
    row_index = lax.broadcasted_iota(jnp.int32, (length, length), 0)
    col_index = lax.broadcasted_iota(jnp.int32, (length, length), 1)
    causal = (row_index >= col_index)[None]
    spread = cumulative.T[:, :, None] - cumulative.T[:, None, :]
    weights = jnp.where(causal, jnp.exp(jnp.where(causal, spread, 0.0)), 0.0)
    return (cumulative, weights)


def forward_shard(head_input, injector, readout, log_decay, start_state):
    length, heads_count = log_decay.shape
    cumulative, weights = decay_table(log_decay)
    intersection = jnp.dot(readout, injector.T, preferred_element_type=jnp.float32)
    mixing = intersection[None] * weights
    inputs_heads = head_input.reshape(length, heads_count, -1).astype(jnp.float32)
    within = jnp.einsum("hts,shp->thp", mixing, inputs_heads, precision=precise)
    carried = jnp.einsum("tn,hpn->thp", readout.astype(jnp.float32), start_state, precision=precise)
    outputs = within + jnp.exp(cumulative)[:, :, None] * carried
    return outputs.reshape(length, -1).astype(jnp.bfloat16)


def chain_piece(readout, output_grad, log_decay):
    length, heads_count = log_decay.shape
    cumulative = jnp.cumsum(log_decay, axis=0)
    grad_heads = output_grad.reshape(length, heads_count, -1).astype(jnp.float32)
    scaled = jnp.exp(cumulative)[:, :, None] * readout.astype(jnp.float32)[:, None, :]
    adjoint = jnp.einsum("thp,thn->hpn", grad_heads, scaled, precision=precise)
    return (jnp.exp(cumulative[-1]), adjoint)


def backward_shard(head_input, injector, readout, output_grad, log_decay, start_state, incoming):
    length, heads_count = log_decay.shape
    cumulative, weights = decay_table(log_decay)
    inputs_narrow = head_input.reshape(length, heads_count, -1)
    grad_narrow = output_grad.reshape(length, heads_count, -1)
    inputs_heads = inputs_narrow.astype(jnp.float32)
    grad_heads = grad_narrow.astype(jnp.float32)
    inject_float = injector.astype(jnp.float32)
    read_float = readout.astype(jnp.float32)
    intersection = jnp.dot(readout, injector.T, preferred_element_type=jnp.float32)
    mixing = intersection[None] * weights
    to_end = jnp.exp(cumulative[-1][None, :] - cumulative)
    from_start = jnp.exp(cumulative)
    entering = jnp.einsum("sn,hpn->shp", inject_float, incoming, precision=precise)
    grad_input = (
        jnp.einsum("hts,thp->shp", mixing, grad_heads, precision=precise)
        + to_end[:, :, None] * entering
    )
    pairing = (
        jnp.einsum("thp,shp->hts", grad_narrow, inputs_narrow, preferred_element_type=jnp.float32)
        * weights
    )
    through_start = jnp.einsum("thp,hpn->thn", grad_heads, start_state, precision=precise)
    grad_read = jnp.einsum("hts,sn->tn", pairing, inject_float, precision=precise)
    grad_read = grad_read + jnp.einsum("th,thn->tn", from_start, through_start, precision=precise)
    input_state = jnp.einsum("shp,hpn->shn", inputs_heads, incoming, precision=precise)
    grad_inject = jnp.einsum("hts,tn->sn", pairing, read_float, precision=precise)
    grad_inject = grad_inject + jnp.einsum("sh,shn->sn", to_end, input_state, precision=precise)
    products = intersection[None] * pairing
    carried = (
        jnp.einsum("tn,hpn->thp", read_float, start_state, precision=precise)
        * from_start[:, :, None]
    )
    reaching = to_end * jnp.einsum("shn,sn->sh", input_state, inject_float, precision=precise)
    end_term = from_start[-1] * jnp.einsum(
        "hpn,hpn->h", incoming, start_state, precision=precise
    ) + jnp.sum(reaching, axis=0)
    cumul_grad = jnp.sum(products, axis=2).T - jnp.sum(products, axis=1).T
    cumul_grad = cumul_grad + jnp.sum(grad_heads * carried, axis=2) - reaching
    is_last = lax.broadcasted_iota(jnp.int32, (length, 1), 0) == length - 1
    cumul_grad = cumul_grad + jnp.where(is_last, end_term[None, :], 0.0)
    decay_grad = jnp.flip(jnp.cumsum(jnp.flip(cumul_grad, 0), axis=0), 0)
    rate_terms = jnp.sum(decay_grad * log_decay, axis=0)
    return (grad_input.reshape(length, -1).astype(jnp.bfloat16), grad_inject, grad_read, rate_terms)


def combine(earlier, later):
    return (later[0] * earlier[0], later[1] + later[0][:, None, None] * earlier[1])


def local(
    cotangent, out_weight, head_input, injector, readout, decay_code, decay_rate, start_state
):
    grad_out = cotangent[0]
    inputs_local = head_input[0]
    inject_local = injector[0]
    read_local = readout[0]
    state_local = start_state[0, 0]
    length = grad_out.shape[0]
    output_grad = lax.dot_general(
        grad_out,
        lax.all_gather(out_weight, "ctx", axis=1, tiled=True),
        (((1,), (1,)), ((), ())),
        preferred_element_type=jnp.float32,
    ).astype(jnp.bfloat16)
    log_decay = -decay_rate[None, :] * decay_code[0].astype(jnp.float32)
    decay_total, adjoint = chain_piece(read_local, output_grad, log_decay)
    identity = (jnp.ones_like(decay_total), jnp.zeros_like(adjoint))
    incoming = carried_in((decay_total, adjoint), "ctx", combine, identity)[1]
    outputs = forward_shard(inputs_local, inject_local, read_local, log_decay, state_local)
    local_weight = lax.dot_general(
        outputs, grad_out, (((0,), (0,)), ((), ())), preferred_element_type=jnp.float32
    )
    data_part = lax.psum_scatter(local_weight, "dp", scatter_dimension=1, tiled=True)
    weight_part = lax.psum_scatter(data_part, "ctx", scatter_dimension=0, tiled=True)
    grad_input, grad_inject, grad_read, rate_terms = backward_shard(
        inputs_local, inject_local, read_local, output_grad, log_decay, state_local, incoming
    )
    tokens_all = length * lax.axis_size("dp") * lax.axis_size("ctx")
    rate_sum = lax.psum(rate_terms, ("dp", "ctx"))
    return (
        grad_input[None],
        grad_inject[None],
        grad_read[None],
        weight_part,
        rate_sum / tokens_all,
    )


def solution(mesh):
    in_specs = (
        P("dp", "ctx", None),
        P(None, "ctx"),
        P("dp", "ctx", None),
        P("dp", "ctx", None),
        P("dp", "ctx", None),
        P("dp", "ctx", None),
        P(),
        P("dp", "ctx", None, None, None),
    )
    out_specs = (
        P("dp", "ctx", None),
        P("dp", "ctx", None),
        P("dp", "ctx", None),
        P("ctx", "dp"),
        P(),
    )
    return jax.shard_map(local, mesh=mesh, in_specs=in_specs, out_specs=out_specs, check_vma=False)
```

profile of v0, /device:TPU:2, one launch (start us, length us, event | category | flops | bytes accessed | tf_op | source)
XLA Modules:
  0.0 262.4 jit_solution(3269358175071123547)
XLA Ops:
  7.2 0.7 all-gather.5.cloned.1.call-update
  7.9 0.7 neg.4
  8.6 0.8 fusion.61
  9.4 0.6 reduce-window.14
  10.3 0.9 bitcast_convert_fusion.1
  11.5 56.1 %all-gather.5.cloned.1.call-done = bf16[256,8192]{1,0:T(8,128)(2,1)} async-done(((bf16[256,1024]{1,0:T(8,128)(2,1)}), bf16[256,8192]{1,0:T(8,128)(2,1)}) %all-gather.5.cloned.1.call-update) | async-done | bytes 4194320 | tf_op jit(solution)/shard_map/all_gather | solution.py:118
  67.6 6.9 %fusion.26 = bf16[512,256]{0,1:T(8,128)(2,1)S(1)} fusion(bf16[256,8192]{1,0:T(8,128)(2,1)} %all-gather.5.cloned.1.call-done, bf16[1,512,8192]{2,1,0:T(8,128)(2,1)} %param.10), kind=kOutput, calls=%fused_computation.24 | convolution fusion | flops 2147614720 | bytes 12845056 | tf_op jit(solution)/shard_map/dot_general | solution.py:116
  74.6 1.1 fusion.43
  76.8 2.0 fusion.22
  78.7 9.1 %fusion.1 = f32[256,8192]{1,0:T(8,128)} fusion(bf16[512,256]{0,1:T(8,128)(2,1)S(1)} %bitcast.164, bf16[1,512,8192]{2,1,0:T(8,128)(2,1)} %param.10), kind=kOutput, calls=%fused_computation.3 | convolution fusion | flops 2147483648 | bytes 17039360 | tf_op jit(solution)/shard_map/dot_general | solution.py:127
  88.0 14.7 %all-gather.1 = f32[8,1,2]{2,1,0:T(1,128)S(1)} all-gather(f32[1,1,2]{2,1,0:T(1,128)S(1)} %bitcast.175), channel_id=1, replica_groups=mesh['dp'=32,'ctx'=8] {'ctx'}, dimensions={0}, use_global_device_ids=true | all-gather | bytes 72 | tf_op jit(solution)/shard_map/all_gather | solution.py:11
  104.0 4.4 %fusion.45 = f32[512,1,128]{2,1,0:T(1,128)} fusion(f32[512,2,1]{1,2,0:T(1,128)S(1)} %copy.72, f32[512,2,128]{2,0,1:T(8,128)S(1)} %convolution_bitcast_fusion), kind=kOutput, calls=%fused_computation.47 | convolution fusion | flops 1572864 | bytes 790528 | tf_op jit(solution)/shard_map/th,thn->tn/dot_general | solution.py:81
  108.4 2.4 fusion.11
  110.8 2.2 multiply_reduce_fusion
  113.1 1.3 rev.13
  114.5 0.9 while.14
  116.6 0.6 reduce-window.16
  118.2 1.3 fusion.29
  119.5 75.2 %psum.7 = f32[2]{0:T(128)S(1)} all-reduce(f32[2]{0:T(128)S(1)} %multiply_reduce_fusion.3), channel_id=1, replica_groups=mesh['dp'=32,'ctx'=8] {'dp','ctx'}, use_global_device_ids=true, to_apply=%region_14.15 | all-reduce | flops 2 | bytes 16 | tf_op jit(solution)/shard_map/psum | solution.py:136
  194.9 21.4 %reduce-scatter.3.cloned.1.call-done = f32[256,256]{1,0:T(8,128)} async-done(((f32[256,8192]{1,0:T(8,128)}), f32[256,256]{1,0:T(8,128)}) %reduce-scatter.3.cloned.1.call-update) | async-done | bytes 262160 | tf_op jit(solution)/shard_map/reduce_scatter | solution.py:130
  216.7 0.8 copy.62
  217.6 1.7 fusion.30
  219.3 0.5 broadcast_multiply_fusion
  219.8 36.1 %reduce-scatter.5.cloned.1.call-done = f32[32,256]{1,0:T(8,128)} async-done(((f32[256,256]{1,0:T(8,128)}), f32[32,256]{1,0:T(8,128)}) %reduce-scatter.5.cloned.1.call-update) | async-done | bytes 32784 | tf_op jit(solution)/shard_map/reduce_scatter | solution.py:131
  (76 shorter events, 6.6 us)
Async XLA Ops:
  7.2 60.4 %all-gather.5.cloned.1.call-start = ((), (), s32[]{:S(2)}) async-start(), calls=%async_computation.2 | async-start | bytes 4718592 | tf_op jit(solution)/shard_map/all_gather | solution.py:118
  7.9 105.2 %all-gather.7.cloned.1.call-start = ((), (), s32[]{:S(2)}) async-start(), calls=%async_computation.5 | async-start | bytes 1179648 | tf_op jit(solution)/shard_map/all_gather | solution.py:11
  11.5 64.2 %copy-start.4 = (bf16[1,512,256]{2,1,0:T(8,128)(2,1)S(1)}, bf16[1,512,256]{2,1,0:T(8,128)(2,1)}, u32[]{:S(2)}) copy-start(bf16[1,512,256]{2,1,0:T(8,128)(2,1)} %param.12) | copy-start | bytes 786436
  11.5 64.5 %copy-start = (bf16[1,512,128]{2,1,0:T(8,128)(2,1)S(1)}, bf16[1,512,128]{2,1,0:T(8,128)(2,1)}, u32[]{:S(2)}) copy-start(bf16[1,512,128]{2,1,0:T(8,128)(2,1)} %param.13) | copy-start | bytes 393220
  11.5 64.5 %copy-start.1 = (bf16[1,512,128]{2,1,0:T(8,128)(2,1)S(1)}, bf16[1,512,128]{2,1,0:T(8,128)(2,1)}, u32[]{:S(2)}) copy-start(bf16[1,512,128]{2,1,0:T(8,128)(2,1)} %param.14) | copy-start | bytes 393220
  74.5 1.8 copy-start.2
  75.7 140.6 %reduce-scatter.3.cloned.1.call-start = ((), (), s32[]{:S(2)}) async-start(), calls=%async_computation.3 | async-start | bytes 8650752 | tf_op jit(solution)/shard_map/reduce_scatter | solution.py:130
  76.0 32.4 %copy-start.5 = (pred[512,512]{1,0:T(8,128)(4,1)}, pred[512,512]{1,0:T(8,128)(4,1)S(1)}, u32[]{:S(2)}) copy-start(pred[512,512]{1,0:T(8,128)(4,1)S(1)} %iota_compare_fusion) | copy-start | bytes 786436
  87.8 168.0 %reduce-scatter.5.cloned.1.call-start = ((), (), s32[]{:S(2)}) async-start(), calls=%async_computation.4 | async-start | bytes 294912 | tf_op jit(solution)/shard_map/reduce_scatter | solution.py:131
  114.4 3.5 %copy-start.7 = (s32[1,512,2]{1,2,0:T(2,128)S(1)}, s32[1,512,2]{1,2,0:T(2,128)}, u32[]{:S(2)}) copy-start(s32[1,512,2]{1,2,0:T(2,128)} %param.15) | copy-start | bytes 12292
  114.5 3.7 %copy-start.6 = (f32[512,1,128]{2,1,0:T(1,128)S(1)}, f32[512,1,128]{2,1,0:T(1,128)}, u32[]{:S(2)}) copy-start(f32[512,1,128]{2,1,0:T(1,128)} %fusion.45) | copy-start | bytes 786436
  115.5 100.8 %copy-start.3 = (f32[512,2,128]{0,2,1:T(8,128)S(1)}, f32[512,2,128]{0,2,1:T(8,128)}, u32[]{:S(2)}) copy-start(f32[512,2,128]{0,2,1:T(8,128)} %fusion.11) | copy-start | bytes 1572868
Sparse Core Ops, SparseCore 0:
  9.8 57.7 all-gather.4
  75.8 37.3 all-gather.6
  117.2 99.0 reduce-scatter.2
  219.4 36.4 reduce-scatter.4
where the time goes:
time: 263 us; the launch traced here: 262 us
  waiting for transfers between devices  114 us (43%)
  blocking collectives  89.9 us (34%)
  matrix products  33.1 us (13%)
  between operations  14 us (5%)
  other arithmetic  5.93 us (2%)
  local copies, waits for them, and re-layouts  4.61 us (2%)
    psum x1, blocking collectives, local(): rate_sum = lax.psum(rate_terms, ('dp', 'ctx'))  75.2 us
    all_gather x1, waiting for transfers between devices, local(): lax.all_gather(out_weight, 'ctx', axis=1, tiled=True)  56.1 us
    reduce_scatter x1, waiting for transfers between devices, local(): lax.psum_scatter(data_part, 'ctx', scatter_dimension=0, tiled=True)  36.1 us
    reduce_scatter x1, waiting for transfers between devices, local(): lax.psum_scatter(local_weight, 'dp', scatter_dimension=1, tiled=True)  21.4 us
    all_gather x1, blocking collectives, carried_in(): pieces = jax.tree.map(lambda part: lax.all_gather(part, axis), value)  14.7 us
    dot_general x1, matrix products, local(): lax.dot_general(outputs, grad_out, (((0,), (0,)), ((), ())), preferred_el...  9.06 us
    dot_general x1, matrix products, local(): lax.dot_general(grad_out, lax.all_gather(out_weight, 'ctx', axis=1, tiled...  6.93 us
  transfers between devices with their start and end apart: 4, of which 4 were waited for; matrix products, arithmetic and copies ran while one was open for 14% of the time, Pallas kernels for 0%

commit v1 on v0

--- a/solution.py
+++ b/solution.py
@@ -115,7 +115,9 @@
     length = grad_out.shape[0]
     output_grad = lax.dot_general(
         grad_out,
-        lax.all_gather(out_weight, "ctx", axis=1, tiled=True),
+        jnp.concatenate(
+            lax.all_to_all(jnp.stack([out_weight] * lax.axis_size("ctx")), "ctx", 0, 0), axis=1
+        ),
         (((1,), (1,)), ((), ())),
         preferred_element_type=jnp.float32,
     ).astype(jnp.bfloat16)

time: 263 us -> 283 us (1.076)
  waiting for transfers between devices: 114 us -> 124 us
  starting transfers between devices: 0.16 us -> 8.72 us
  local copies, waits for them, and re-layouts: 4.61 us -> 8.15 us
    all_to_all x0 -> x1, waiting for transfers between devices: none -> 95 us  [local(): lax.all_to_all(jnp.stack([out_weight] * lax.axis_size('ctx')), 'ctx', 0, 0)]
    all_gather x1 -> x0, waiting for transfers between devices: 56.1 us -> none  [local(): lax.all_gather(out_weight, 'ctx', axis=1, tiled=True)]
    reduce_scatter x1, waiting for transfers between devices: 21.4 us -> 0.03 us  [local(): lax.psum_scatter(local_weight, 'dp', scatter_dimension=1, tiled=True)]
    all_to_all x0 -> x1, starting transfers between devices: none -> 8.6 us  [local(): lax.all_to_all(jnp.stack([out_weight] * lax.axis_size('ctx')), 'ctx', 0, 0)]
    reduce_scatter x1, waiting for transfers between devices: 36.1 us -> 29.2 us  [local(): lax.psum_scatter(data_part, 'ctx', scatter_dimension=0, tiled=True)]
  transfers between devices with their start and end apart: 4 -> 4, of which waited for: 4 -> 2; matrix products, arithmetic and copies ran while one was open for 14% -> 12% of each run, Pallas kernels for 0% -> 0%
where the time goes in v1:
time: 283 us
  waiting for transfers between devices  124 us (44%)
  blocking collectives  88.1 us (31%)
  matrix products  34 us (12%)
  between operations  15.7 us (6%)
  starting transfers between devices  8.72 us (3%)
  local copies, waits for them, and re-layouts  8.15 us (3%)
  other arithmetic  3.66 us (1%)
    all_to_all x1, waiting for transfers between devices, local(): lax.all_to_all(jnp.stack([out_weight] * lax.axis_size('ctx')), 'ctx', 0, 0)  95 us
    psum x1, blocking collectives, local(): rate_sum = lax.psum(rate_terms, ('dp', 'ctx'))  74.3 us
    reduce_scatter x1, waiting for transfers between devices, local(): lax.psum_scatter(data_part, 'ctx', scatter_dimension=0, tiled=True)  29.2 us
    all_gather x1, blocking collectives, carried_in(): pieces = jax.tree.map(lambda part: lax.all_gather(part, axis), value)  13.8 us
    dot_general x1, matrix products, local(): lax.dot_general(outputs, grad_out, (((0,), (0,)), ((), ())), preferred_el...  8.95 us
    all_to_all x1, starting transfers between devices, local(): lax.all_to_all(jnp.stack([out_weight] * lax.axis_size('ctx')), 'ctx', 0, 0)  8.6 us
    dot_general x1, matrix products, local(): lax.dot_general(grad_out, jnp.concatenate(lax.all_to_all(jnp.stack([out_w...  6.99 us
  transfers between devices with their start and end apart: 4, of which 2 were waited for; matrix products, arithmetic and copies ran while one was open for 12% of the time, Pallas kernels for 0%

profile of v1, /device:TPU:2, one launch (start us, length us, event | category | flops | bytes accessed | tf_op | source)
XLA Modules:
  0.0 282.9 jit_solution(13713077421960301664)
XLA Ops:
  8.0 1.2 copy.54
  9.2 2.2 stack.2
  11.5 8.6 %all-to-all-start = ((bf16[8,256,1024]{1,2,0:T(8,128)(2,1)}), bf16[8,256,1024]{1,2,0:T(8,128)(2,1)}, u32[]{:S(2)}, u32[]{:S(2)}) async-start(bf16[8,256,1024]{1,2,0:T(8,128)(2,1)} %stack.2), calls=%async_computation | async-start | bytes 8388608 | tf_op jit(solution)/shard_map/all_to_all | solution.py:119
  20.3 0.6 reduce-window.14
  21.4 95.0 %all-to-all-done = bf16[8,256,1024]{1,2,0:T(8,128)(2,1)} async-done(((bf16[8,256,1024]{1,2,0:T(8,128)(2,1)}), bf16[8,256,1024]{1,2,0:T(8,128)(2,1)}, u32[]{:S(2)}, u32[]{:S(2)}) %all-to-all-start) | async-done | bytes 4194336 | tf_op jit(solution)/shard_map/all_to_all | solution.py:119
  116.5 7.0 %fusion.26 = bf16[512,256]{0,1:T(8,128)(2,1)S(1)} fusion(bf16[256,8192]{0,1:T(8,128)(2,1)} %bitcast.5, bf16[1,512,8192]{2,1,0:T(8,128)(2,1)} %param.10), kind=kOutput, calls=%fused_computation.24 | convolution fusion | flops 2147614720 | bytes 12845056 | tf_op jit(solution)/shard_map/dot_general | solution.py:116
  123.5 1.1 fusion.43
  125.2 0.4 multiply_reduce_fusion.2
  125.7 2.0 fusion.22
  127.7 9.0 %fusion.1 = f32[256,8192]{1,0:T(8,128)} fusion(bf16[512,256]{0,1:T(8,128)(2,1)S(1)} %bitcast.167, bf16[1,512,8192]{2,1,0:T(8,128)(2,1)} %param.10), kind=kOutput, calls=%fused_computation.3 | convolution fusion | flops 2147483648 | bytes 17039360 | tf_op jit(solution)/shard_map/dot_general | solution.py:129
  136.9 13.8 %all-gather.1 = f32[8,1,2]{2,1,0:T(1,128)S(1)} all-gather(f32[1,1,2]{2,1,0:T(1,128)S(1)} %bitcast.178), channel_id=1, replica_groups=mesh['dp'=32,'ctx'=8] {'ctx'}, dimensions={0}, use_global_device_ids=true | all-gather | bytes 72 | tf_op jit(solution)/shard_map/all_gather | solution.py:11
  151.9 4.4 %fusion.45 = f32[512,1,128]{2,1,0:T(1,128)} fusion(f32[512,2,1]{1,2,0:T(1,128)S(1)} %copy.75, f32[512,2,128]{2,0,1:T(8,128)S(1)} %convolution_bitcast_fusion), kind=kOutput, calls=%fused_computation.47 | convolution fusion | flops 1572864 | bytes 790528 | tf_op jit(solution)/shard_map/th,thn->tn/dot_general | solution.py:81
  156.3 2.4 fusion.11
  158.7 2.2 multiply_reduce_fusion
  160.9 1.4 rev.13
  162.3 0.9 while.14
  163.3 0.4 fusion.41
  164.4 0.6 reduce-window.16
  166.0 2.3 fusion.29
  168.2 74.3 %psum.7 = f32[2]{0:T(128)S(1)} all-reduce(f32[2]{0:T(128)S(1)} %multiply_reduce_fusion.3), channel_id=1, replica_groups=mesh['dp'=32,'ctx'=8] {'dp','ctx'}, use_global_device_ids=true, to_apply=%region_14.15 | all-reduce | flops 2 | bytes 16 | tf_op jit(solution)/shard_map/psum | solution.py:138
  243.2 0.8 copy.65
  244.0 1.7 fusion.30
  245.7 0.5 broadcast_multiply_fusion
  246.2 29.2 %reduce-scatter.5.cloned.1.call-done = f32[32,256]{1,0:T(8,128)} async-done(((f32[256,256]{1,0:T(8,128)}), f32[32,256]{1,0:T(8,128)}) %reduce-scatter.5.cloned.1.call-update) | async-done | bytes 32784 | tf_op jit(solution)/shard_map/reduce_scatter | solution.py:133
  (77 shorter events, 5.7 us)
Async XLA Ops:
  11.5 8.6 %copy-start.7 = (f32[2]{0:T(128)S(1)}, f32[2]{0:T(128)}, u32[]{:S(2)}) copy-start(f32[2]{0:T(128)} %param.16) | copy-start | bytes 28
  11.5 8.7 %copy-start.6 = (s32[1,512,2]{1,2,0:T(2,128)S(1)}, s32[1,512,2]{1,2,0:T(2,128)}, u32[]{:S(2)}) copy-start(s32[1,512,2]{1,2,0:T(2,128)} %param.15) | copy-start | bytes 12292
  11.5 9.7 %copy-start.1 = (bf16[1,512,128]{2,1,0:T(8,128)(2,1)S(1)}, bf16[1,512,128]{2,1,0:T(8,128)(2,1)}, u32[]{:S(2)}) copy-start(bf16[1,512,128]{2,1,0:T(8,128)(2,1)} %param.14) | copy-start | bytes 393220
  11.5 105.0 %all-to-all-start = ((bf16[8,256,1024]{1,2,0:T(8,128)(2,1)}), bf16[8,256,1024]{1,2,0:T(8,128)(2,1)}, u32[]{:S(2)}, u32[]{:S(2)}) async-start(bf16[8,256,1024]{1,2,0:T(8,128)(2,1)} %stack.2), calls=%async_computation | async-start | bytes 8388608 | tf_op jit(solution)/shard_map/all_to_all | solution.py:119
  20.1 140.8 %all-gather.4.cloned.1.call-start = ((), (), s32[]{:S(2)}) async-start(), calls=%async_computation.5 | async-start | bytes 1179648 | tf_op jit(solution)/shard_map/all_gather | solution.py:11
  116.5 8.2 %copy-start.4 = (bf16[1,512,256]{2,1,0:T(8,128)(2,1)S(1)}, bf16[1,512,256]{2,1,0:T(8,128)(2,1)}, u32[]{:S(2)}) copy-start(bf16[1,512,256]{2,1,0:T(8,128)(2,1)} %param.12) | copy-start | bytes 786436
  116.5 8.4 %copy-start = (bf16[1,512,128]{2,1,0:T(8,128)(2,1)S(1)}, bf16[1,512,128]{2,1,0:T(8,128)(2,1)}, u32[]{:S(2)}) copy-start(bf16[1,512,128]{2,1,0:T(8,128)(2,1)} %param.13) | copy-start | bytes 393220
  123.5 1.7 copy-start.2
  124.6 118.1 %reduce-scatter.3.cloned.1.call-start = ((), (), s32[]{:S(2)}) async-start(), calls=%async_computation.3 | async-start | bytes 8650752 | tf_op jit(solution)/shard_map/reduce_scatter | solution.py:132
  124.9 31.4 %copy-start.5 = (pred[512,512]{1,0:T(8,128)(4,1)}, pred[512,512]{1,0:T(8,128)(4,1)S(1)}, u32[]{:S(2)}) copy-start(pred[512,512]{1,0:T(8,128)(4,1)S(1)} %iota_compare_fusion) | copy-start | bytes 786436
  136.6 138.8 %reduce-scatter.5.cloned.1.call-start = ((), (), s32[]{:S(2)}) async-start(), calls=%async_computation.4 | async-start | bytes 294912 | tf_op jit(solution)/shard_map/reduce_scatter | solution.py:133
  163.3 79.5 %copy-start.3 = (f32[512,2,128]{0,2,1:T(8,128)S(1)}, f32[512,2,128]{0,2,1:T(8,128)}, u32[]{:S(2)}) copy-start(f32[512,2,128]{0,2,1:T(8,128)} %fusion.11) | copy-start | bytes 1572868
Sparse Core Ops, SparseCore 0:
  124.7 35.0 all-gather.3
  242.9 32.5 reduce-scatter.4
Sparse Core Ops, SparseCore 1:
  136.7 96.3 reduce-scatter.2
